TPU v7x, 128 devices: a whole 4x4x4 slice. The times are simulated.
128 devices in a mesh: row: 8 (over x, z_hi), col: 16 (over y, z_lo, core).
Axes of the slice: x: 4, y: 4, z: 4 (z_hi: 2, z_lo: 2; z = z_hi * 2 + z_lo), core: 2. Of those that a mesh axis runs over, the one named last changes fastest.
Arguments:
- points: float32 [8, 131072], P(None, ('row', 'col')), may hold values from -4 to 4
- point_order: int32 [128, 1024], P(('row', 'col')), may hold values from 0 to 1023, each once within a row
- noise_var: float32 [131072], P(('row', 'col')), may hold values from 0.1 to 3
- inv_scale: float32 [8], replicated, may hold values from 0.2 to 0.6
- basis_vectors: float32 [16, 64, 131072], P(None, None, ('row', 'col')), may hold values from -4 to 4
- current: float32 [64, 131072], P(None, ('row', 'col')), may hold values from -22 to 22
- tile_rows: int32 [8, 16, 64], P('row', 'col'), may hold values from 0 to 63, as said below
- tile_cols: int32 [8, 16, 64], P('row', 'col'), may hold values from 0 to 31
Outputs:
- lanczos_next: float32 [64, 131072], P(None, ('row', 'col'))
- coefficients: float32 [4, 64], replicated
- gradient_product: float32 [64, 131072], P(None, ('row', 'col'))
Inputs may be any that keep to these rules, and one draw needn't show every extreme that they name: In each grid cell the 64 pairs (tile_rows, tile_cols) are distinct; each cell lists its 4 pairs with I = J; over all cells no unordered pair of distinct blocks is listed twice: it is listed as (I, J) with I < J when I + J is odd and with I > J when I + J is even.
All inputs are finite; a program needn't handle non-finite values.
Results may differ from a plain program's by a relative error of at most 0.00019.
Values sent between devices are 32-bit elements; how exact they have to be, the bound alone decides.
No kernel may reach another device: no remote copies, remote signals or barrier semaphores. Data moves between devices by JAX's collectives and lax.ppermute only.
A program may use at most 128 MiB of HBM per device.

v0:
```python
import math
import jax
import jax.numpy as jnp
from jax import lax
from jax.sharding import PartitionSpec as P

BLOCK = 256
ITERS = 2
ROOT_THREE = math.sqrt(3.0)
SUPPORT = 3.0
EPSILON = 1e-06
HIGHEST = lax.Precision.HIGHEST


def kernel_tiles(row_points, col_points):
    dist_sq = jnp.zeros(
        (row_points.shape[1], row_points.shape[2], col_points.shape[2]), jnp.float32
    )
    for feature in range(row_points.shape[0]):
        differ = row_points[feature][:, :, None] - col_points[feature][:, None, :]
        dist_sq = dist_sq + differ * differ
    shifted = dist_sq + EPSILON
    radius = jnp.sqrt(shifted)
    decaying = jnp.exp(-ROOT_THREE * radius)
    matern_part = (1.0 + ROOT_THREE * radius) * decaying
    tapered = jnp.maximum(1.0 - radius / SUPPORT, 0.0)
    taper_cube = tapered * tapered * tapered
    weight = taper_cube * tapered * (1.0 + 4.0 * radius / SUPPORT)
    kernel_tile = matern_part * weight
    slope_tile = shifted * (
        3.0 * decaying * weight + 20.0 * matern_part * taper_cube / (SUPPORT * SUPPORT)
    )
    return (kernel_tile, slope_tile)


def tile_products(
    col_values, row_values, col_points, row_points, row_blocks, col_blocks, mirror_mask, with_slope
):
    probe_count = col_values.shape[0]
    block_len = col_values.shape[2]
    group_size = math.gcd(row_blocks.shape[0], 8)
    layers = 2 if with_slope else 1
    row_total = jnp.zeros((layers, probe_count, row_values.shape[1], block_len), jnp.float32)
    col_total = jnp.zeros((layers, probe_count, col_values.shape[1], block_len), jnp.float32)
    grouped = (
        row_blocks.reshape(-1, group_size),
        col_blocks.reshape(-1, group_size),
        mirror_mask.reshape(-1, group_size),
    )

    def one_group(carried, listed):
        row_acc, col_acc = carried
        row_pick, col_pick, mirror_pick = listed
        kernel_tile, slope_tile = kernel_tiles(
            jnp.take(row_points, row_pick, axis=1), jnp.take(col_points, col_pick, axis=1)
        )
        if with_slope:
            stacked = jnp.stack([kernel_tile, slope_tile])
        else:
            stacked = kernel_tile[None]
        col_side = jnp.take(col_values, col_pick, axis=1)
        row_side = jnp.take(row_values, row_pick, axis=1) * mirror_pick[None, :, None]
        direct = jnp.einsum("pgj,kgij->kpgi", col_side, stacked, precision=HIGHEST)
        mirrored = jnp.einsum("pgi,kgij->kpgj", row_side, stacked, precision=HIGHEST)
        return (
            (row_acc.at[:, :, row_pick].add(direct), col_acc.at[:, :, col_pick].add(mirrored)),
            None,
        )

    (row_total, col_total), unused = lax.scan(one_group, (row_total, col_total), grouped)
    return (
        row_total.reshape(layers * probe_count, -1),
        col_total.reshape(layers * probe_count, -1),
    )


def both_sides(stacked):
    col_side = lax.all_gather(stacked, "row", axis=1, tiled=True)
    row_side = lax.all_gather(stacked, "col", axis=1, tiled=True)
    return (col_side, row_side)


def reduce_parts(row_part, col_part):
    from_rows = lax.psum_scatter(row_part, "col", scatter_dimension=1, tiled=True)
    from_cols = lax.psum_scatter(col_part, "row", scatter_dimension=1, tiled=True)
    return from_rows + from_cols


def on_device(
    points, point_order, noise_var, inv_scale, basis_vectors, current, tile_rows, tile_cols
):
    feature_count = points.shape[0]
    probe_count = current.shape[0]
    per_device = points.shape[1]
    block_count = per_device // BLOCK
    row_count = lax.axis_size("row")
    col_count = lax.axis_size("col")
    point_total = per_device * row_count * col_count
    arrangement = point_order[0]
    scaled = jnp.take(points, arrangement, axis=1) * inv_scale[:, None]
    noise_here = jnp.take(noise_var, arrangement)
    row_blocks = tile_rows[0, 0]
    col_blocks = tile_cols[0, 0]
    global_row = lax.axis_index("row") * col_count * block_count + row_blocks
    global_col = (
        col_blocks // block_count * col_count + lax.axis_index("col")
    ) * block_count + col_blocks % block_count
    mirror_mask = (global_row != global_col).astype(jnp.float32)
    earlier = basis_vectors
    coefficient_rows = []
    gradient_product = current
    col_points = scaled
    row_points = scaled
    for iteration in range(ITERS):
        if iteration == 0:
            stacked = jnp.concatenate([scaled, current], axis=0)
            apply_col_side, apply_row_side = both_sides(stacked)
            apply_col_points = apply_col_side[:feature_count].reshape(feature_count, -1, BLOCK)
            apply_row_points = apply_row_side[:feature_count].reshape(feature_count, -1, BLOCK)
            apply_row_part, apply_col_part = tile_products(
                apply_col_side[feature_count:].reshape(probe_count, -1, BLOCK),
                apply_row_side[feature_count:].reshape(probe_count, -1, BLOCK),
                apply_col_points,
                apply_row_points,
                row_blocks,
                col_blocks,
                mirror_mask,
                True,
            )
            summed = reduce_parts(apply_row_part, apply_col_part)
            image_vec = summed[:probe_count] + noise_here * current
            gradient_product = summed[probe_count:]
            col_points = apply_col_points
            row_points = apply_row_points
        else:
            col_side, row_side = both_sides(current)
            row_part, col_part = tile_products(
                col_side.reshape(probe_count, -1, BLOCK),
                row_side.reshape(probe_count, -1, BLOCK),
                col_points,
                row_points,
                row_blocks,
                col_blocks,
                mirror_mask,
                False,
            )
            image_vec = reduce_parts(row_part, col_part) + noise_here * current
        earlier_dots, alpha_now = lax.psum(
            (
                jnp.einsum("hpn,pn->hp", earlier, image_vec, precision=HIGHEST),
                jnp.sum(current * image_vec, axis=1),
            ),
            ("row", "col"),
        )
        earlier_dots = earlier_dots / point_total
        alpha_now = alpha_now / point_total
        residual_vec = (
            image_vec
            - alpha_now[:, None] * current
            - jnp.einsum("hp,hpn->pn", earlier_dots, earlier, precision=HIGHEST)
        )
        residual_sq = (
            lax.psum(jnp.sum(residual_vec * residual_vec, axis=1), ("row", "col")) / point_total
        )
        beta_now = jnp.sqrt(residual_sq + EPSILON)
        coefficient_rows += [alpha_now, beta_now]
        if iteration + 1 < ITERS:
            earlier = jnp.concatenate([earlier, current[None]], axis=0)
        current = residual_vec / beta_now[:, None]
    return (current, jnp.stack(coefficient_rows), gradient_product)


def solution(mesh):
    return jax.shard_map(
        on_device,
        mesh=mesh,
        in_specs=(
            P(None, ("row", "col")),
            P(("row", "col"), None),
            P(("row", "col")),
            P(),
            P(None, None, ("row", "col")),
            P(None, ("row", "col")),
            P("row", "col", None),
            P("row", "col", None),
        ),
        out_specs=(P(None, ("row", "col")), P(), P(None, ("row", "col"))),
        check_vma=False,
    )
```

profile of v0, /device:TPU:1, one launch (start us, length us, event | category | flops | bytes accessed | tf_op | source)
XLA Modules:
  0.0 1346.3 jit_solution(8351384830638760810)
XLA Ops:
  17.7 55.4 %all-gather.7.cloned.1.call-done = f32[72,8192]{1,0:T(8,128)} async-done(((f32[72,1024]{1,0:T(8,128)}), f32[72,8192]{1,0:T(8,128)}) %all-gather.7.cloned.1.call-update) | async-done | bytes 2359312 | tf_op jit(solution)/shard_map/all_gather | solution.py:78
  76.3 36.9 %all-gather.5.cloned.1.call-done = f32[72,16384]{1,0:T(8,128)} async-done(((f32[72,1024]{1,0:T(8,128)}), f32[72,16384]{1,0:T(8,128)}) %all-gather.5.cloned.1.call-update) | async-done | bytes 4718608 | tf_op jit(solution)/shard_map/all_gather | solution.py:79
  127.0 261.6 %while.30 = (s32[]{:T(128)}, f32[2,64,64,256]{3,1,2,0:T(8,128)}, f32[2,64,32,256]{3,1,2,0:T(8,128)}, s32[8,8]{1,0:T(8,128)S(1)}, f32[8,64,256]{2,0,1:T(8,128)}, ...) while((s32[]{:T(128)}, f32[2,64,64,256]{3,1,2,0:T(8,128)}, ...), condition=%wide.region_3.8_spmd, body=%wide.region_0.7_spmd.sunk | while | flops 1637255296 | bytes 25305864 | solution.py:70
  129.6 5.7 fusion.113
  139.6 4.5 fusion.116
  150.4 5.9 fusion.114
  162.2 5.7 fusion.113
  172.2 4.5 fusion.116
  183.1 5.9 fusion.114
  195.0 5.7 fusion.113
  204.9 4.5 fusion.116
  215.7 5.9 fusion.114
  227.6 5.7 fusion.113
  237.6 4.5 fusion.116
  248.4 5.9 fusion.114
  260.3 5.7 fusion.113
  281.0 5.9 fusion.114
  292.9 5.7 fusion.113
  313.7 5.9 fusion.114
  325.6 5.7 fusion.113
  335.6 4.5 fusion.116
  346.4 5.9 fusion.114
  358.3 5.7 fusion.113
  379.1 5.9 fusion.114
  388.6 4.6 copy.34
  393.2 5.4 copy.88
  398.7 8.2 copy.33
  406.9 9.7 copy.87
  416.7 12.2 all-gather.9.cloned.1.call-start
  429.0 4.5 gather_fusion.9
  433.5 49.1 %reduce-scatter.7.cloned.1.call-done = f32[128,1024]{1,0:T(8,128)} async-done(((f32[128,8192]{1,0:T(8,128)}), f32[128,1024]{1,0:T(8,128)}) %reduce-scatter.7.cloned.1.call-update) | async-done | bytes 524304 | tf_op jit(solution)/shard_map/reduce_scatter | solution.py:85
  482.6 99.5 %reduce-scatter.5.cloned.1.call-done = f32[128,1024]{1,0:T(8,128)} async-done(((f32[128,16384]{1,0:T(8,128)}), f32[128,1024]{1,0:T(8,128)}) %reduce-scatter.5.cloned.1.call-update) | async-done | bytes 524304 | tf_op jit(solution)/shard_map/reduce_scatter | solution.py:84
  583.6 9.0 fusion.67
  592.5 65.6 %all-reduce.1 = (f32[16,64]{0,1:T(8,128)S(1)}, f32[64]{0:T(128)S(1)}) all-reduce(f32[16,64]{0,1:T(8,128)S(1)} %bitcast.438, f32[64]{0:T(128)S(1)} %get-tuple-element.445), channel_id=1, replica_groups=mesh['row'=8,'col'=16] {'row','col'}, use_global_device_ids=true, to_apply=%region_8.13 | all-reduce | flops 1088 | bytes 8704 | tf_op jit(solution)/shard_map/psum | solution.py:148
  658.2 6.5 fusion.65
  666.1 63.1 %psum.44 = f32[64]{0:T(128)S(1)} all-reduce(f32[64]{0:T(128)S(1)} %get-tuple-element.401), channel_id=1, replica_groups=mesh['row'=8,'col'=16] {'row','col'}, use_global_device_ids=true, to_apply=%region_10.15 | all-reduce | flops 64 | bytes 512 | tf_op jit(solution)/shard_map/psum | solution.py:163
  731.3 49.9 %all-gather.9.cloned.1.call-done = f32[64,8192]{1,0:T(8,128)} async-done(((f32[64,1024]{1,0:T(8,128)}), f32[64,8192]{1,0:T(8,128)}) %all-gather.9.cloned.1.call-update) | async-done | bytes 2097168 | tf_op jit(solution)/shard_map/all_gather | solution.py:78
  784.5 36.7 %all-gather.11.cloned.1.call-done = f32[64,16384]{1,0:T(8,128)} async-done(((f32[64,1024]{1,0:T(8,128)}), f32[64,16384]{1,0:T(8,128)}) %all-gather.11.cloned.1.call-update) | async-done | bytes 4194320 | tf_op jit(solution)/shard_map/all_gather | solution.py:79
  821.2 4.9 copy.177
  828.8 214.8 %while.31 = (s32[]{:T(128)}, f32[1,64,64,256]{3,1,2,0:T(8,128)}, f32[1,64,32,256]{3,1,2,0:T(8,128)S(1)}, s32[8,8]{1,0:T(8,128)S(1)}, f32[8,64,256]{2,0,1:T(8,128...) while((s32[]{:T(128)}, f32[1,64,64,256]{3,1,2,0:T(8,128)}, ...), condition=%wide.region_14.19_spmd, body=%wide.region_11.18_spmd.sunk | while | flops 845842560 | bytes 8660057 | solution.py:70
  835.0 7.2 convolution_bitcast_fusion.5
  845.9 7.0 convolution_bitcast_fusion.4
  861.8 7.2 convolution_bitcast_fusion.5
  872.8 7.0 convolution_bitcast_fusion.4
  888.7 7.2 convolution_bitcast_fusion.5
  899.7 7.0 convolution_bitcast_fusion.4
  915.5 7.2 convolution_bitcast_fusion.5
  926.5 7.0 convolution_bitcast_fusion.4
  942.4 7.2 convolution_bitcast_fusion.5
  953.3 7.0 convolution_bitcast_fusion.4
  969.2 7.2 convolution_bitcast_fusion.5
  980.2 7.0 convolution_bitcast_fusion.4
  996.1 7.2 convolution_bitcast_fusion.5
  1007.0 7.0 convolution_bitcast_fusion.4
  1022.9 7.2 convolution_bitcast_fusion.5
  1033.9 7.0 convolution_bitcast_fusion.4
  1045.4 4.6 copy.89
  1051.0 4.9 pad_maximum_fusion.7
  1056.0 64.1 %reduce-scatter.11.cloned.1.call-done = f32[64,1024]{1,0:T(8,128)} async-done(((f32[64,8192]{1,0:T(8,128)}), f32[64,1024]{1,0:T(8,128)}) %reduce-scatter.11.cloned.1.call-update) | async-done | bytes 262160 | tf_op jit(solution)/shard_map/reduce_scatter | solution.py:85
  1120.1 67.1 %reduce-scatter.9.cloned.1.call-done = f32[64,1024]{1,0:T(8,128)} async-done(((f32[64,16384]{1,0:T(8,128)}), f32[64,1024]{1,0:T(8,128)}) %reduce-scatter.9.cloned.1.call-update) | async-done | bytes 262160 | tf_op jit(solution)/shard_map/reduce_scatter | solution.py:84
  1188.5 10.2 fusion.63
  1198.7 68.3 %all-reduce = (f32[17,64]{0,1:T(8,128)S(1)}, f32[64]{0:T(128)S(1)}) all-reduce(f32[17,64]{0,1:T(8,128)S(1)} %bitcast.439, f32[64]{0:T(128)S(1)} %get-tuple-element.399), channel_id=1, replica_groups=mesh['row'=8,'col'=16] {'row','col'}, use_global_device_ids=true, to_apply=%region_19.24 | all-reduce | flops 1152 | bytes 9216 | tf_op jit(solution)/shard_map/psum | solution.py:148
  1267.0 7.8 fusion.61
  1275.1 62.6 %psum.47 = f32[64]{0:T(128)S(1)} all-reduce(f32[64]{0:T(128)S(1)} %get-tuple-element.397), channel_id=1, replica_groups=mesh['row'=8,'col'=16] {'row','col'}, use_global_device_ids=true, to_apply=%region_21.26 | all-reduce | flops 64 | bytes 512 | tf_op jit(solution)/shard_map/psum | solution.py:163
  (653 shorter events, 287.5 us)
Async XLA Ops:
  7.2 421.8 %copy-start = (f32[1024]{0:T(1024)S(1)}, f32[1024]{0:T(1024)}, u32[]{:S(2)}) copy-start(f32[1024]{0:T(1024)} %param.22) | copy-start | bytes 12292
  7.2 6.3 copy-start.4
  7.2 8.4 copy-start.18
  7.2 9.1 copy-start.19
  7.2 65.9 %all-gather.7.cloned.1.call-start = ((), (), s32[]{:S(2)}) async-start(), calls=%async_computation.5 | async-start | bytes 2654208 | tf_op jit(solution)/shard_map/all_gather | solution.py:78
  14.3 98.8 %all-gather.5.cloned.1.call-start = ((), (), s32[]{:S(2)}) async-start(), calls=%async_computation.4 | async-start | bytes 5013504 | tf_op jit(solution)/shard_map/all_gather | solution.py:79
  15.0 467.6 %reduce-scatter.7.cloned.1.call-start = ((), (), s32[]{:S(2)}) async-start(), calls=%async_computation.7 | async-start | bytes 4718592 | tf_op jit(solution)/shard_map/reduce_scatter | solution.py:85
  73.1 1.6 slice-start
  124.5 2.5 slice-start.1
  398.6 183.5 %reduce-scatter.5.cloned.1.call-start = ((), (), s32[]{:S(2)}) async-start(), calls=%async_computation.6 | async-start | bytes 8912896 | tf_op jit(solution)/shard_map/reduce_scatter | solution.py:84
  416.7 16.8 %copy-start.13 = (s32[1,1024]{1,0:T(1,128)S(1)}, s32[1,1024]{1,0:T(1,128)}, u32[]{:S(2)}) copy-start(s32[1,1024]{1,0:T(1,128)} %param.21) | copy-start | bytes 12292
  416.7 166.7 %copy-start.5 = (f32[64,1024]{1,0:T(8,128)S(1)}, f32[64,1024]{1,0:T(8,128)}, u32[]{:S(2)}) copy-start(f32[64,1024]{1,0:T(8,128)} %param.25) | copy-start | bytes 786436
  416.7 364.5 %all-gather.9.cloned.1.call-start = ((), (), s32[]{:S(2)}) async-start(), calls=%async_computation.8 | async-start | bytes 2359296 | tf_op jit(solution)/shard_map/all_gather | solution.py:78
  433.5 231.7 %copy-start.7 = (f32[1,1024]{1,0:T(1,128)}, f32[1,1024]{1,0:T(1,128)S(1)}, u32[]{:S(2)}) copy-start(f32[1,1024]{1,0:T(1,128)S(1)} %and_select_fusion) | copy-start | bytes 12292
  666.1 118.4 %copy-start.2 = (f32[64,1024]{1,0:T(8,128)}, f32[64,1024]{1,0:T(8,128)S(1)}, u32[]{:S(2)}) copy-start(f32[64,1024]{1,0:T(8,128)S(1)} %get-tuple-element.402) | copy-start | bytes 786436
  729.8 54.6 %copy-start.14 = (f32[64]{0:T(128)}, f32[64]{0:T(128)S(1)}, u32[]{:S(2)}) copy-start(f32[64]{0:T(128)S(1)} %get-tuple-element.451) | copy-start | bytes 772
  730.6 90.6 %all-gather.11.cloned.1.call-start = ((), (), s32[]{:S(2)}) async-start(), calls=%async_computation.9 | async-start | bytes 4456448 | tf_op jit(solution)/shard_map/all_gather | solution.py:79
  731.2 388.9 %reduce-scatter.11.cloned.1.call-start = ((), (), s32[]{:S(2)}) async-start(), calls=%async_computation.11 | async-start | bytes 2359296 | tf_op jit(solution)/shard_map/reduce_scatter | solution.py:85
  828.9 1.8 copy-start.11
  828.9 2.6 copy-start.9
  842.7 3.2 copy-start.10
  845.9 7.0 copy-start.12
  855.7 1.8 copy-start.11
  855.7 2.6 copy-start.9
  869.5 3.2 copy-start.10
  872.8 7.0 copy-start.12
  882.6 1.8 copy-start.11
  882.6 2.6 copy-start.9
  896.4 3.2 copy-start.10
  899.6 7.0 copy-start.12
  909.4 1.8 copy-start.11
  909.4 2.6 copy-start.9
  923.3 3.2 copy-start.10
  926.5 7.0 copy-start.12
  936.2 1.8 copy-start.11
  936.3 2.6 copy-start.9
  950.1 3.2 copy-start.10
  953.3 7.0 copy-start.12
  963.1 1.8 copy-start.11
  963.1 2.6 copy-start.9
  976.9 3.2 copy-start.10
  980.2 7.0 copy-start.12
  989.9 1.8 copy-start.11
  989.9 2.6 copy-start.9
  1003.8 3.2 copy-start.10
  1007.0 7.0 copy-start.12
  1016.8 1.8 copy-start.11
  1016.8 2.6 copy-start.9
  1030.6 3.2 copy-start.10
  1033.9 7.0 copy-start.12
  1045.2 142.1 %reduce-scatter.9.cloned.1.call-start = ((), (), s32[]{:S(2)}) async-start(), calls=%async_computation.10 | async-start | bytes 4456448 | tf_op jit(solution)/shard_map/reduce_scatter | solution.py:84
  1050.1 0.9 copy-start.6
  1051.0 136.2 %copy-start.3 = (f32[64,1024]{1,0:T(8,128)S(1)}, f32[64,1024]{1,0:T(8,128)}, u32[]{:S(2)}) copy-start(f32[64,1024]{1,0:T(8,128)} %copy-done.2) | copy-start | bytes 786436
  1051.0 136.2 %copy-start.8 = (f32[1,1024]{1,0:T(1,128)S(1)}, f32[1,1024]{1,0:T(1,128)}, u32[]{:S(2)}) copy-start(f32[1,1024]{1,0:T(1,128)} %copy-done.7) | copy-start | bytes 12292
  1051.0 136.2 %copy-start.15 = (f32[64]{0:T(128)S(1)}, f32[64]{0:T(128)}, u32[]{:S(2)}) copy-start(f32[64]{0:T(128)} %copy-done.14) | copy-start | bytes 772
  1267.0 71.6 %copy-start.16 = (f32[1,64]{1,0:T(1,128)S(1)}, f32[1,64]{1,0:T(1,128)}, u32[]{:S(2)}) copy-start(f32[1,64]{1,0:T(1,128)} %get-tuple-element.448) | copy-start | bytes 772
  1267.0 71.6 %copy-start.17 = (f32[1,64]{1,0:T(1,128)S(1)}, f32[1,64]{1,0:T(1,128)}, u32[]{:S(2)}) copy-start(f32[1,64]{1,0:T(1,128)} %get-tuple-element.450) | copy-start | bytes 772
  1267.0 72.1 %copy-start.1 = (f32[1024]{0:T(1024)S(1)}, f32[1024]{0:T(1024)}, u32[]{:S(2)}) copy-start(f32[1024]{0:T(1024)} %param.22) | copy-start | bytes 12292
Sparse Core Ops, SparseCore 0:
  14.4 58.6 all-gather.6
  74.7 38.3 all-gather.4
  398.8 83.8 reduce-scatter.6
  484.9 97.2 reduce-scatter.4
  730.8 50.4 all-gather.8
  783.3 37.8 all-gather.10
  1045.3 74.7 reduce-scatter.10
  1122.5 64.6 reduce-scatter.8
where the time goes:
time: 1360 us; the launch traced here: 1350 us
  waiting for transfers between devices  460 us (34%)
  blocking collectives  260 us (19%)
  matrix products  230 us (17%)
  local copies, waits for them, and re-layouts  212 us (16%)
  other arithmetic  153 us (11%)
  between operations  14.8 us (1%)
    reduce_scatter x2, waiting for transfers between devices, reduce_parts(): lax.psum_scatter(row_part, 'col', scatter_dimension=1, tiled=True)  167 us
    psum x2, blocking collectives, on_device(): lax.psum((jnp.einsum('hpn,pn->hp', earlier, image_vec, precision=HIGHEST)...  134 us
    psum x2, blocking collectives, on_device(): lax.psum(jnp.sum(residual_vec * residual_vec, axis=1), ('row', 'col'))  126 us
    reduce_scatter x2, waiting for transfers between devices, reduce_parts(): lax.psum_scatter(col_part, 'row', scatter_dimension=1, tiled=True)  113 us
    all_gather x2, waiting for transfers between devices, both_sides(): col_side = lax.all_gather(stacked, 'row', axis=1, tiled=True)  105 us
    dot_general x16, matrix products, one_group(): direct = jnp.einsum('pgj,kgij->kpgi', col_side, stacked, precision=HIGHEST)  103 us
    dot_general x16, matrix products, one_group(): jnp.einsum('pgi,kgij->kpgj', row_side, stacked, precision=HIGHEST)  93.6 us
    all_gather x2, waiting for transfers between devices, both_sides(): row_side = lax.all_gather(stacked, 'col', axis=1, tiled=True)  73.6 us
  transfers between devices with their start and end apart: 8, of which 8 were waited for; matrix products, arithmetic and copies ran while one was open for 3% of the time, Pallas kernels for 0%

commit v1 on v0

--- a/solution.py
+++ b/solution.py
@@ -75,7 +75,9 @@
 
 
 def both_sides(stacked):
-    col_side = lax.all_gather(stacked, "row", axis=1, tiled=True)
+    col_side = jnp.concatenate(
+        lax.all_to_all(jnp.stack([stacked] * lax.axis_size("row")), "row", 0, 0), axis=1
+    )
     row_side = lax.all_gather(stacked, "col", axis=1, tiled=True)
     return (col_side, row_side)
 

time: 1360 us -> 1280 us (0.941)
  waiting for transfers between devices: 460 us -> 347 us
  blocking collectives: 260 us -> 295 us
    all_gather x2 -> x0, waiting for transfers between devices: 105 us -> none  [both_sides(): col_side = lax.all_gather(stacked, 'row', axis=1, tiled=True)]
    all_gather x2, waiting for transfers between devices: 73.6 us -> 21.4 us  [both_sides(): row_side = lax.all_gather(stacked, 'col', axis=1, tiled=True)]
    all_to_all x0 -> x1, blocking collectives: none -> 35.4 us  [both_sides(): lax.all_to_all(jnp.stack([stacked] * lax.axis_size('row')), 'row', 0, 0)]
    all_to_all x0 -> x1, waiting for transfers between devices: none -> 32.2 us  [both_sides(): lax.all_to_all(jnp.stack([stacked] * lax.axis_size('row')), 'row', 0, 0)]
    gather x16, local copies, waits for them, and re-layouts: 25.5 us -> 8.88 us  [one_group(): jnp.take(row_points, row_pick, axis=1)]
    gather x16, local copies, waits for them, and re-layouts: 8.88 us -> 24 us  [one_group(): jnp.take(col_points, col_pick, axis=1)]
  transfers between devices with their start and end apart: 8 -> 7, of which waited for: 8 -> 7; matrix products, arithmetic and copies ran while one was open for 3% -> 4% of each run, Pallas kernels for 0% -> 0%
where the time goes in v1:
time: 1280 us; the launch traced here: 1270 us
  waiting for transfers between devices  347 us (27%)
  blocking collectives  295 us (23%)
  matrix products  231 us (18%)
  local copies, waits for them, and re-layouts  216 us (17%)
  other arithmetic  154 us (12%)
  between operations  14.6 us (1%)
    reduce_scatter x2, waiting for transfers between devices, reduce_parts(): lax.psum_scatter(row_part, 'col', scatter_dimension=1, tiled=True)  167 us
    psum x2, blocking collectives, on_device(): lax.psum((jnp.einsum('hpn,pn->hp', earlier, image_vec, precision=HIGHEST)...  134 us
    reduce_scatter x2, waiting for transfers between devices, reduce_parts(): lax.psum_scatter(col_part, 'row', scatter_dimension=1, tiled=True)  127 us
    psum x2, blocking collectives, on_device(): lax.psum(jnp.sum(residual_vec * residual_vec, axis=1), ('row', 'col'))  126 us
    dot_general x16, matrix products, one_group(): direct = jnp.einsum('pgj,kgij->kpgi', col_side, stacked, precision=HIGHEST)  103 us
    dot_general x16, matrix products, one_group(): jnp.einsum('pgi,kgij->kpgj', row_side, stacked, precision=HIGHEST)  93.7 us
    gather x16, local copies, waits for them, and re-layouts, one_group(): jnp.take(row_values, row_pick, axis=1) * mirror_pick[None, :, None]  50.6 us
    scatter-add x16, other arithmetic, one_group(): row_acc.at[:, :, row_pick].add(direct)  48.4 us
  transfers between devices with their start and end apart: 7, of which 7 were waited for; matrix products, arithmetic and copies ran while one was open for 4% of the time, Pallas kernels for 0%

profile of v1, /device:TPU:1, one launch (start us, length us, event | category | flops | bytes accessed | tf_op | source)
XLA Modules:
  0.0 1270.0 jit_solution(4878872235146117051)
XLA Ops:
  16.9 8.3 all-to-all-start
  27.3 32.2 %all-to-all-done = f32[8,72,1024]{2,1,0:T(8,128)S(1)} async-done(((f32[8,72,1024]{2,1,0:T(8,128)}), f32[8,72,1024]{2,1,0:T(8,128)S(1)}, u32[]{:S(2)}, u32[]{:S(2)}) %all-to-all-start) | async-done | bytes 2359328 | tf_op jit(solution)/shard_map/all_to_all | solution.py:79
  67.8 11.4 all-gather.3.cloned.1.call-done
  91.0 255.9 %while.30 = (s32[]{:T(128)}, f32[2,64,64,256]{3,1,2,0:T(8,128)}, f32[2,64,32,256]{3,1,2,0:T(8,128)}, s32[8,8]{1,0:T(8,128)S(1)}, f32[8,64,256]{2,0,1:T(8,128)S(1...) while((s32[]{:T(128)}, f32[2,64,64,256]{3,1,2,0:T(8,128)}, ...), condition=%wide.region_3.8_spmd, body=%wide.region_0.7_spmd.sunk | while | flops 1637255296 | bytes 29500224 | solution.py:70
  93.6 5.7 fusion.113
  102.9 4.5 fusion.116
  113.7 5.9 fusion.114
  125.4 5.7 fusion.113
  134.7 4.5 fusion.116
  145.6 5.9 fusion.114
  157.4 5.7 fusion.113
  166.7 4.5 fusion.116
  177.5 5.9 fusion.114
  189.3 5.7 fusion.113
  198.6 4.5 fusion.116
  209.4 5.9 fusion.114
  221.2 5.7 fusion.113
  241.4 5.9 fusion.114
  253.2 5.7 fusion.113
  262.5 4.5 fusion.116
  273.4 5.9 fusion.114
  285.2 5.7 fusion.113
  305.3 5.9 fusion.114
  317.1 5.7 fusion.113
  337.3 5.9 fusion.114
  346.9 4.8 copy.58
  351.7 5.3 copy.112
  357.1 8.2 copy.57
  365.3 9.7 copy.111
  375.3 4.5 gather_fusion.9
  379.9 61.3 %reduce-scatter.7.cloned.1.call-done = f32[128,1024]{1,0:T(8,128)} async-done(((f32[128,8192]{1,0:T(8,128)}), f32[128,1024]{1,0:T(8,128)}) %reduce-scatter.7.cloned.1.call-update) | async-done | bytes 524304 | tf_op jit(solution)/shard_map/reduce_scatter | solution.py:87
  441.2 99.7 %reduce-scatter.5.cloned.1.call-done = f32[128,1024]{1,0:T(8,128)} async-done(((f32[128,16384]{1,0:T(8,128)}), f32[128,1024]{1,0:T(8,128)}) %reduce-scatter.5.cloned.1.call-update) | async-done | bytes 524304 | tf_op jit(solution)/shard_map/reduce_scatter | solution.py:86
  542.3 9.0 fusion.67
  551.3 65.7 %all-reduce.1 = (f32[16,64]{0,1:T(8,128)S(1)}, f32[64]{0:T(128)S(1)}) all-reduce(f32[16,64]{0,1:T(8,128)S(1)} %bitcast.432, f32[64]{0:T(128)S(1)} %get-tuple-element.485), channel_id=1, replica_groups=mesh['row'=8,'col'=16] {'row','col'}, use_global_device_ids=true, to_apply=%region_8.13 | all-reduce | flops 1088 | bytes 8704 | tf_op jit(solution)/shard_map/psum | solution.py:150
  617.0 6.5 fusion.65
  625.0 63.0 %psum.44 = f32[64]{0:T(128)S(1)} all-reduce(f32[64]{0:T(128)S(1)} %get-tuple-element.441), channel_id=1, replica_groups=mesh['row'=8,'col'=16] {'row','col'}, use_global_device_ids=true, to_apply=%region_10.15 | all-reduce | flops 64 | bytes 512 | tf_op jit(solution)/shard_map/psum | solution.py:165
  690.7 35.4 %all_to_all.10 = f32[8,64,1024]{2,1,0:T(8,128)S(1)} all-to-all(f32[8,64,1024]{2,1,0:T(8,128)S(1)} %stack.24), channel_id=1, replica_groups=mesh['row'=8,'col'=16] {'row'}, dimensions={0} | all-to-all | bytes 4194304 | tf_op jit(solution)/shard_map/all_to_all | solution.py:79
  733.2 10.0 all-gather.5.cloned.1.call-done
  743.1 4.8 copy.199
  751.4 215.1 %while.31 = (s32[]{:T(128)}, f32[1,64,64,256]{3,1,2,0:T(8,128)}, f32[1,64,32,256]{3,1,2,0:T(8,128)S(1)}, s32[8,8]{1,0:T(8,128)S(1)}, f32[8,64,256]{2,0,1:T(8,128...) while((s32[]{:T(128)}, f32[1,64,64,256]{3,1,2,0:T(8,128)}, ...), condition=%wide.region_14.19_spmd, body=%wide.region_11.18_spmd.sunk | while | flops 845842560 | bytes 10759349 | solution.py:70
  757.5 7.2 convolution_bitcast_fusion.5
  768.6 7.0 convolution_bitcast_fusion.4
  784.4 7.2 convolution_bitcast_fusion.5
  795.4 7.0 convolution_bitcast_fusion.4
  811.3 7.2 convolution_bitcast_fusion.5
  822.4 7.0 convolution_bitcast_fusion.4
  838.2 7.2 convolution_bitcast_fusion.5
  849.3 7.0 convolution_bitcast_fusion.4
  865.1 7.2 convolution_bitcast_fusion.5
  876.1 7.0 convolution_bitcast_fusion.4
  891.9 7.2 convolution_bitcast_fusion.5
  903.0 7.0 convolution_bitcast_fusion.4
  918.8 7.2 convolution_bitcast_fusion.5
  929.9 7.0 convolution_bitcast_fusion.4
  945.7 7.2 convolution_bitcast_fusion.5
  956.8 7.0 convolution_bitcast_fusion.4
  968.1 4.6 copy.113
  973.7 4.9 pad_maximum_fusion.7
  978.6 65.2 %reduce-scatter.11.cloned.1.call-done = f32[64,1024]{1,0:T(8,128)} async-done(((f32[64,8192]{1,0:T(8,128)}), f32[64,1024]{1,0:T(8,128)}) %reduce-scatter.11.cloned.1.call-update) | async-done | bytes 262160 | tf_op jit(solution)/shard_map/reduce_scatter | solution.py:87
  1043.8 66.9 %reduce-scatter.9.cloned.1.call-done = f32[64,1024]{1,0:T(8,128)} async-done(((f32[64,16384]{1,0:T(8,128)}), f32[64,1024]{1,0:T(8,128)}) %reduce-scatter.9.cloned.1.call-update) | async-done | bytes 262160 | tf_op jit(solution)/shard_map/reduce_scatter | solution.py:86
  1112.0 10.2 fusion.63
  1122.2 68.5 %all-reduce = (f32[17,64]{0,1:T(8,128)S(1)}, f32[64]{0:T(128)S(1)}) all-reduce(f32[17,64]{0,1:T(8,128)S(1)} %bitcast.433, f32[64]{0:T(128)S(1)} %get-tuple-element.439), channel_id=1, replica_groups=mesh['row'=8,'col'=16] {'row','col'}, use_global_device_ids=true, to_apply=%region_19.24 | all-reduce | flops 1152 | bytes 9216 | tf_op jit(solution)/shard_map/psum | solution.py:150
  1190.8 7.8 fusion.61
  1198.9 62.6 %psum.47 = f32[64]{0:T(128)S(1)} all-reduce(f32[64]{0:T(128)S(1)} %get-tuple-element.437), channel_id=1, replica_groups=mesh['row'=8,'col'=16] {'row','col'}, use_global_device_ids=true, to_apply=%region_21.26 | all-reduce | flops 64 | bytes 512 | tf_op jit(solution)/shard_map/psum | solution.py:165
  (735 shorter events, 290.8 us)
Async XLA Ops:
  7.2 368.1 %copy-start = (f32[1024]{0:T(1024)S(1)}, f32[1024]{0:T(1024)}, u32[]{:S(2)}) copy-start(f32[1024]{0:T(1024)} %param.22) | copy-start | bytes 12292
  7.2 6.3 copy-start.7
  7.2 72.0 %all-gather.3.cloned.1.call-start = ((), (), s32[]{:S(2)}) async-start(), calls=%async_computation.6 | async-start | bytes 5013504 | tf_op jit(solution)/shard_map/all_gather | solution.py:81
  16.9 8.8 copy-start.23
  16.9 9.6 copy-start.24
  16.9 42.6 %all-to-all-start = ((f32[8,72,1024]{2,1,0:T(8,128)}), f32[8,72,1024]{2,1,0:T(8,128)S(1)}, u32[]{:S(2)}, u32[]{:S(2)}) async-start(f32[8,72,1024]{2,1,0:T(8,128)} %stack.23), calls=%async_computation | async-start | bytes 4718592 | tf_op jit(solution)/shard_map/all_to_all | solution.py:79
  25.2 416.0 %reduce-scatter.7.cloned.1.call-start = ((), (), s32[]{:S(2)}) async-start(), calls=%async_computation.8 | async-start | bytes 4718592 | tf_op jit(solution)/shard_map/reduce_scatter | solution.py:87
  91.0 2.5 copy-start.2
  119.6 3.3 copy-start.3
  122.9 2.5 copy-start.2
  151.5 3.4 copy-start.3
  154.9 2.5 copy-start.2
  183.4 3.3 copy-start.3
  215.3 3.3 copy-start.3
  247.3 3.3 copy-start.3
  279.3 3.3 copy-start.3
  311.2 3.4 copy-start.3
  343.2 3.3 copy-start.3
  346.9 4.8 copy-start.4
  357.0 183.9 %reduce-scatter.5.cloned.1.call-start = ((), (), s32[]{:S(2)}) async-start(), calls=%async_computation.7 | async-start | bytes 8912896 | tf_op jit(solution)/shard_map/reduce_scatter | solution.py:86
  375.1 4.8 copy-start.16
  375.1 368.1 %all-gather.5.cloned.1.call-start = ((), (), s32[]{:S(2)}) async-start(), calls=%async_computation.9 | async-start | bytes 4456448 | tf_op jit(solution)/shard_map/all_gather | solution.py:81
  379.9 244.2 %copy-start.10 = (f32[1,1024]{1,0:T(1,128)}, f32[1,1024]{1,0:T(1,128)S(1)}, u32[]{:S(2)}) copy-start(f32[1,1024]{1,0:T(1,128)S(1)} %and_select_fusion) | copy-start | bytes 12292
  617.0 7.1 copy-start.8
  688.6 37.5 %copy-start.17 = (f32[64]{0:T(128)}, f32[64]{0:T(128)S(1)}, u32[]{:S(2)}) copy-start(f32[64]{0:T(128)S(1)} %get-tuple-element.491) | copy-start | bytes 772
  689.4 354.4 %reduce-scatter.11.cloned.1.call-start = ((), (), s32[]{:S(2)}) async-start(), calls=%async_computation.11 | async-start | bytes 2359296 | tf_op jit(solution)/shard_map/reduce_scatter | solution.py:87
  765.3 3.2 copy-start.13
  768.5 7.1 copy-start.15
  775.6 2.7 copy-start.6
  775.6 2.7 copy-start.20
  792.2 3.2 copy-start.13
  795.4 7.1 copy-start.15
  802.5 2.8 copy-start.6
  802.5 2.8 copy-start.20
  819.1 3.2 copy-start.13
  822.4 7.1 copy-start.15
  829.4 2.7 copy-start.6
  829.4 2.7 copy-start.20
  846.0 3.2 copy-start.13
  849.2 7.0 copy-start.15
  856.3 2.7 copy-start.6
  856.3 2.7 copy-start.20
  872.9 3.2 copy-start.13
  876.1 7.0 copy-start.15
  883.1 2.8 copy-start.6
  883.1 2.8 copy-start.20
  899.8 3.2 copy-start.13
  903.0 7.1 copy-start.15
  910.0 2.7 copy-start.6
  910.0 2.7 copy-start.20
  926.7 3.2 copy-start.13
  929.9 7.0 copy-start.15
  936.9 2.7 copy-start.6
  936.9 2.7 copy-start.20
  953.5 3.2 copy-start.13
  956.8 7.0 copy-start.15
  963.8 2.8 copy-start.6
  963.8 2.8 copy-start.20
  968.1 142.6 %reduce-scatter.9.cloned.1.call-start = ((), (), s32[]{:S(2)}) async-start(), calls=%async_computation.10 | async-start | bytes 4456448 | tf_op jit(solution)/shard_map/reduce_scatter | solution.py:86
  973.7 137.0 %copy-start.11 = (f32[1,1024]{1,0:T(1,128)S(1)}, f32[1,1024]{1,0:T(1,128)}, u32[]{:S(2)}) copy-start(f32[1,1024]{1,0:T(1,128)} %copy-done.10) | copy-start | bytes 12292
  973.7 137.0 %copy-start.18 = (f32[64]{0:T(128)S(1)}, f32[64]{0:T(128)}, u32[]{:S(2)}) copy-start(f32[64]{0:T(128)} %copy-done.17) | copy-start | bytes 772
  1190.8 71.5 %copy-start.21 = (f32[1,64]{1,0:T(1,128)S(1)}, f32[1,64]{1,0:T(1,128)}, u32[]{:S(2)}) copy-start(f32[1,64]{1,0:T(1,128)} %get-tuple-element.488) | copy-start | bytes 772
  1190.8 71.5 %copy-start.22 = (f32[1,64]{1,0:T(1,128)S(1)}, f32[1,64]{1,0:T(1,128)}, u32[]{:S(2)}) copy-start(f32[1,64]{1,0:T(1,128)} %get-tuple-element.490) | copy-start | bytes 772
  1190.8 72.1 %copy-start.1 = (f32[1024]{0:T(1024)S(1)}, f32[1024]{0:T(1024)}, u32[]{:S(2)}) copy-start(f32[1024]{0:T(1024)} %param.22) | copy-start | bytes 12292
  (32 other events, 49.0 us)
Sparse Core Ops, SparseCore 0:
  14.4 64.7 all-gather.2
  357.2 84.0 reduce-scatter.6
  443.6 97.2 reduce-scatter.4
  689.5 53.5 all-gather.4
  968.2 75.5 reduce-scatter.10
  1046.1 64.6 reduce-scatter.8
